TPU v7x, 32 devices: a whole 2x2x4 slice. The times are simulated.
32 devices in a mesh: layer: 4 (over z), row: 2 (over x), col: 4 (over y, core).
Axes of the slice: x: 2, y: 2, z: 4, core: 2. Of those that a mesh axis runs over, the one named last changes fastest.
Arguments:
- cost_vector: float32 [8, 1024, 512], P('layer', 'row', 'col'), may hold values from -12 to 12
- metal_density: float32 [8, 1024, 512], P('layer', 'row', 'col'), may hold values from 0 to 0.5
- cap_class: int32 [8, 1024, 512], P('layer', 'row', 'col'), may hold values from 0 to 7
- blocked_mask: int32 [8, 1024, 512], P('layer', 'row', 'col'), may hold values 0 or 1
- fill_start: float32 [8, 1024, 512], P('layer', 'row', 'col'), may hold values from 0 to 1
- window_dual: float32 [8, 1024, 512], P('layer', 'row', 'col'), may hold values from -4 to 4
- layer_dual: float32 [8, 1024, 512], P('layer', 'row', 'col'), may hold values from -4 to 4
Outputs:
- fill_level: float32 [8, 1024, 512], P('layer', 'row', 'col')
- window_price: float32 [8, 1024, 512], P('layer', 'row', 'col')
- layer_price: float32 [8, 1024, 512], P('layer', 'row', 'col')
- primal_weight: float32 [], replicated
All inputs are finite; a program needn't handle non-finite values. No bound on the sum of `blocked_mask` on one device may be relied on, other than what follows from the above.
Results may differ from a plain program's by a relative error of at most 0.00011.
Values sent between devices are 32-bit elements; how exact they have to be, the bound alone decides.
A program may use at most 64 MiB of HBM per device.

v0:
```python
import jax
import jax.numpy as jnp
from jax import lax
from jax.sharding import PartitionSpec as P

WIN = 50
CAP_LEVELS = 8
ITERS = 3


step_eta = 0.4
low_density = 0.35
high_density = 0.65
layer_gap = 0.15
tiny_term = 1e-06


def extended(cells, sides, width):
    for axis, dim in sides:
        count = lax.axis_size(axis)
        ends = count - 1
        head = lax.slice_in_dim(cells, 0, width, axis=dim)
        tail = lax.slice_in_dim(cells, cells.shape[dim] - width, cells.shape[dim], axis=dim)
        cells = jnp.concatenate(
            [
                lax.ppermute(tail, axis, [(i, (i + 1) % count) for i in range(ends)]),
                cells,
                lax.ppermute(head, axis, [((i + 1) % count, i) for i in range(ends)]),
            ],
            axis=dim,
        )
    return cells


def from_behind(block, axis, distance):
    devices = range(lax.axis_size(axis))
    route = [(i - distance, i) for i in devices if i - distance in devices]
    return lax.ppermute(block, axis, route)


def band_matrix(extent_out, extent_in, offset):
    index_out = lax.broadcasted_iota(jnp.int32, (extent_out, extent_in), 0)
    index_in = lax.broadcasted_iota(jnp.int32, (extent_out, extent_in), 1)
    spread = index_in - index_out
    return ((spread >= offset) & (spread < offset + WIN)).astype(jnp.float32)


def rows_pass(row_band, padded):
    return jnp.einsum("ip,lpq->liq", row_band, padded, precision=lax.Precision.HIGHEST)


def cols_pass(partial_sum, col_band):
    return jnp.einsum("liq,qj->lij", partial_sum, col_band, precision=lax.Precision.HIGHEST)


def fill_window(level, row_band, col_band, halfway):
    tall = extended(level, (("row", 1),), halfway)
    partial_sum = rows_pass(row_band, tall)
    wide = extended(partial_sum, (("col", 2),), halfway)
    result = cols_pass(wide, col_band)
    return result


def dual_window(density_dual, row_band, col_band, halfway):
    tall = extended(density_dual, (("row", 1),), halfway)
    partial_sum = rows_pass(row_band, tall)
    wide = extended(partial_sum, (("col", 2),), halfway)
    result = cols_pass(wide, col_band)
    return result


def local(cost_vector, metal_density, cap_class, blocked_mask, fill_start, window_dual, layer_dual):
    layers_here, row_count, col_count = fill_start.shape
    halfway = WIN // 2
    inverse_area = 1.0 / (WIN * WIN)
    row_forward = band_matrix(row_count, row_count + 2 * halfway, 0)
    row_backward = band_matrix(row_count, row_count + 2 * halfway, 1)
    col_forward = band_matrix(col_count, col_count + 2 * halfway, 0).T
    col_backward = band_matrix(col_count, col_count + 2 * halfway, 1).T
    layer_ids = lax.axis_index("layer") * layers_here + lax.iota(jnp.int32, layers_here)
    keep_mask = (layer_ids < lax.axis_size("layer") * layers_here - 1).astype(jnp.float32)[
        :, None, None
    ]
    capacity = jnp.where(blocked_mask == 1, 0.0, (cap_class + 1).astype(jnp.float32) / CAP_LEVELS)
    has_floor = blocked_mask == 0
    filling = fill_start
    density_dual = window_dual
    stacked_dual = layer_dual * keep_mask
    weight = jnp.float32(1.0)
    for iteration in range(ITERS):
        primal_step = step_eta / weight
        dual_step = step_eta * weight
        below = from_behind(stacked_dual[layers_here - 1 :], "layer", 1)
        earlier = jnp.concatenate([below, stacked_dual[: layers_here - 1]], axis=0)
        transposed = dual_window(density_dual, row_backward, col_backward, halfway)
        gradient = cost_vector + transposed * inverse_area + (stacked_dual - earlier)
        fill_new = jnp.clip(filling - primal_step * gradient, 0.0, capacity)
        moved = fill_new - filling
        primal_sum = jnp.sum(moved * moved)
        level = fill_new + moved + metal_density
        above = from_behind(level[0:1], "layer", -1)
        later = jnp.concatenate([level[1:], above], axis=0)
        forward = fill_window(level, row_forward, col_forward, halfway)
        window_term = density_dual / dual_step + forward * inverse_area
        capped = jnp.minimum(window_term, high_density)
        clipped = jnp.where(has_floor, jnp.maximum(capped, low_density), capped)
        density_new = dual_step * (window_term - clipped)
        layer_term = stacked_dual / dual_step + keep_mask * (level - later)
        stacked_new = (
            dual_step * (layer_term - jnp.clip(layer_term, -layer_gap, layer_gap)) * keep_mask
        )
        density_move = density_new - density_dual
        stacked_move = stacked_new - stacked_dual
        dual_sum = jnp.sum(density_move * density_move) + jnp.sum(stacked_move * stacked_move)
        primal_sum, dual_sum = lax.psum((primal_sum, dual_sum), ("layer", "row", "col"))
        weight = jnp.sqrt(weight) * jnp.sqrt(
            jnp.sqrt((dual_sum + tiny_term) / (primal_sum + tiny_term))
        )
        filling = fill_new
        density_dual = density_new
        stacked_dual = stacked_new
    return (filling, density_dual, stacked_dual, weight)


def solution(mesh):
    in_specs = (
        P("layer", "row", "col"),
        P("layer", "row", "col"),
        P("layer", "row", "col"),
        P("layer", "row", "col"),
        P("layer", "row", "col"),
        P("layer", "row", "col"),
        P("layer", "row", "col"),
    )
    out_specs = (P("layer", "row", "col"), P("layer", "row", "col"), P("layer", "row", "col"), P())
    return jax.shard_map(local, mesh=mesh, in_specs=in_specs, out_specs=out_specs, check_vma=False)
```

profile of v0, /device:TPU:0, one launch (start us, length us, event | category | flops | bytes accessed | tf_op | source)
XLA Modules:
  0.0 268.0 jit_solution(12571616555059935040)
XLA Ops:
  1.4 4.9 %collective-permute-start = (f32[2,25,128]{2,1,0:T(8,128)S(1)}, f32[2,25,128]{2,1,0:T(8,128)S(1)}, u32[]{:S(2)}, u32[]{:S(2)}) collective-permute-start(f32[2,25,128]{2,1,0:T(8,128)S(1)} %get-tuple-element.56), channel_id=1, source_target_pairs={{0,4},{1,5},{2,6},{3,7},{8,12},{9,13},{10,14},{11,15},{16,20},{17,... | collective-permute-start | bytes 76808 | tf_op jit(solution)/shard_map/ppermute | solution.py:26
  8.8 3.6 %collective-permute-start.4 = (f32[1,512,128]{2,1,0:T(8,128)S(1)}, f32[1,512,128]{2,1,0:T(8,128)S(1)}, u32[]{:S(2)}, u32[]{:S(2)}) collective-permute-start(f32[1,512,128]{2,1,0:T(8,128)S(1)} %get-tuple-element.52), channel_id=1, source_target_pairs={{0,8},{8,16},{16,24},{1,9},{9,17},{17,25},{2,10},{10,18},{18,26},{... | collective-permute-start | bytes 786440 | tf_op jit(solution)/shard_map/ppermute | solution.py:38
  16.2 3.7 %collective-permute-done.3 = f32[2,512,25]{1,2,0:T(8,128)S(1)} collective-permute-done((f32[2,512,25]{1,2,0:T(8,128)S(1)}, f32[2,512,25]{1,2,0:T(8,128)S(1)}, u32[]{:S(2)}, u32[]{:S(2)}) %collective-permute-start.3) | collective-permute-done | bytes 102432 | tf_op jit(solution)/shard_map/ppermute | solution.py:28
  20.0 2.5 multiply_reduce_fusion.6
  22.5 4.5 %collective-permute-start.5 = (f32[2,25,128]{2,1,0:T(8,128)S(1)}, f32[2,25,128]{2,1,0:T(8,128)S(1)}, u32[]{:S(2)}, u32[]{:S(2)}) collective-permute-start(f32[2,25,128]{2,1,0:T(8,128)S(1)} %get-tuple-element.50), channel_id=1, source_target_pairs={{0,4},{1,5},{2,6},{3,7},{8,12},{9,13},{10,14},{11,15},{16,20},{17,... | collective-permute-start | bytes 76808 | tf_op jit(solution)/shard_map/ppermute | solution.py:26
  28.6 4.2 %collective-permute-done.6 = f32[2,25,128]{2,1,0:T(8,128)S(1)} collective-permute-done((f32[2,25,128]{2,1,0:T(8,128)S(1)}, f32[2,25,128]{2,1,0:T(8,128)S(1)}, u32[]{:S(2)}, u32[]{:S(2)}) %collective-permute-start.6) | collective-permute-done | bytes 25632 | tf_op jit(solution)/shard_map/ppermute | solution.py:28
  33.8 4.0 %collective-permute-start.7 = (f32[2,512,25]{1,2,0:T(8,128)S(1)}, f32[2,512,25]{1,2,0:T(8,128)S(1)}, u32[]{:S(2)}, u32[]{:S(2)}) collective-permute-start(f32[2,512,25]{1,2,0:T(8,128)S(1)} %get-tuple-element.48), channel_id=1, source_target_pairs={{0,1},{1,2},{2,3},{4,5},{5,6},{6,7},{8,9},{9,10},{10,11},{12,13},{... | collective-permute-start | bytes 307208 | tf_op jit(solution)/shard_map/ppermute | solution.py:26
  46.8 4.2 %collective-permute-done.11 = f32[2,25,128]{2,1,0:T(8,128)S(1)} collective-permute-done((f32[2,25,128]{2,1,0:T(8,128)S(1)}, f32[2,25,128]{2,1,0:T(8,128)S(1)}, u32[]{:S(2)}, u32[]{:S(2)}) %collective-permute-start.11) | collective-permute-done | bytes 25632 | tf_op jit(solution)/shard_map/ppermute | solution.py:28
  52.9 3.5 %collective-permute-start.14 = (f32[1,512,128]{2,1,0:T(8,128)S(1)}, f32[1,512,128]{2,1,0:T(8,128)S(1)}, u32[]{:S(2)}, u32[]{:S(2)}) collective-permute-start(f32[1,512,128]{2,1,0:T(8,128)S(1)} %get-tuple-element.40), channel_id=1, source_target_pairs={{0,8},{8,16},{16,24},{1,9},{9,17},{17,25},{2,10},{10,18},{18,26},{... | collective-permute-start | bytes 786440 | tf_op jit(solution)/shard_map/ppermute | solution.py:38
  57.2 4.7 %collective-permute-start.12 = (f32[2,512,25]{1,2,0:T(8,128)}, f32[2,512,25]{1,2,0:T(8,128)}, u32[]{:S(2)}, u32[]{:S(2)}) collective-permute-start(f32[2,512,25]{1,2,0:T(8,128)} %get-tuple-element.44), channel_id=1, source_target_pairs={{0,1},{1,2},{2,3},{4,5},{5,6},{6,7},{8,9},{9,10},{10,11},{12,13},{... | collective-permute-start | bytes 307208 | tf_op jit(solution)/shard_map/ppermute | solution.py:26
  64.4 40.6 %all-reduce.2 = (f32[]{:T(128)}, f32[]{:T(128)}) all-reduce(f32[]{:T(128)S(6)} %add.115, f32[]{:T(128)} %get-tuple-element.20), channel_id=1, replica_groups=mesh['layer'=4,'row'=2,'col'=4] {'layer','row','col'}, use_global_device_ids=true, to_apply=%region_2.3 | all-reduce | flops 2 | bytes 16 | tf_op jit(solution)/shard_map/psum | solution.py:115
  107.2 3.9 %multiply_reduce_fusion.3 = (f32[]{:T(128)}, f32[2,512,128]{2,1,0:T(8,128)S(1)}, f32[2,512,128]{2,1,0:T(8,128)}) fusion(f32[2,512,128]{2,1,0:T(8,128)} %get-tuple-element.58, f32[2,512,128]{2,1,0:T(8,128)S(1)} %copy-done.1, f32[2,512,128]{2,1,0:T(8,128)S(1)} %get-tuple-element.15, f32[1,512,128]{2,1,0:T(8,128)S(1)} %get-tuple-element.41, ...), kind=kOutput, calls=%fused_computation.139 | convolution fusion | flops 282915840 | bytes 5447688 | tf_op jit(solution)/shard_map/liq,qj->lij/dot_general | solution.py:53
  111.1 4.2 %collective-permute-start.15 = (f32[2,25,128]{2,1,0:T(8,128)S(1)}, f32[2,25,128]{2,1,0:T(8,128)S(1)}, u32[]{:S(2)}, u32[]{:S(2)}) collective-permute-start(f32[2,25,128]{2,1,0:T(8,128)S(1)} %get-tuple-element.38), channel_id=1, source_target_pairs={{0,4},{1,5},{2,6},{3,7},{8,12},{9,13},{10,14},{11,15},{16,20},{17,... | collective-permute-start | bytes 76808 | tf_op jit(solution)/shard_map/ppermute | solution.py:26
  116.8 4.2 %collective-permute-done.16 = f32[2,25,128]{2,1,0:T(8,128)S(1)} collective-permute-done((f32[2,25,128]{2,1,0:T(8,128)S(1)}, f32[2,25,128]{2,1,0:T(8,128)S(1)}, u32[]{:S(2)}, u32[]{:S(2)}) %collective-permute-start.16) | collective-permute-done | bytes 25632 | tf_op jit(solution)/shard_map/ppermute | solution.py:28
  126.1 2.9 %collective-permute-done.18 = f32[2,512,25]{1,2,0:T(8,128)S(1)} collective-permute-done((f32[2,512,25]{1,2,0:T(8,128)S(1)}, f32[2,512,25]{1,2,0:T(8,128)S(1)}, u32[]{:S(2)}, u32[]{:S(2)}) %collective-permute-start.18) | collective-permute-done | bytes 102432 | tf_op jit(solution)/shard_map/ppermute | solution.py:28
  134.0 4.2 %collective-permute-done.21 = f32[2,25,128]{2,1,0:T(8,128)S(1)} collective-permute-done((f32[2,25,128]{2,1,0:T(8,128)S(1)}, f32[2,25,128]{2,1,0:T(8,128)S(1)}, u32[]{:S(2)}, u32[]{:S(2)}) %collective-permute-start.21) | collective-permute-done | bytes 25632 | tf_op jit(solution)/shard_map/ppermute | solution.py:28
  143.3 4.7 %collective-permute-start.22 = (f32[2,512,25]{1,2,0:T(8,128)}, f32[2,512,25]{1,2,0:T(8,128)}, u32[]{:S(2)}, u32[]{:S(2)}) collective-permute-start(f32[2,512,25]{1,2,0:T(8,128)} %get-tuple-element.32), channel_id=1, source_target_pairs={{0,1},{1,2},{2,3},{4,5},{5,6},{6,7},{8,9},{9,10},{10,11},{12,13},{... | collective-permute-start | bytes 307208 | tf_op jit(solution)/shard_map/ppermute | solution.py:26
  150.6 40.6 %all-reduce.1 = (f32[]{:T(128)}, f32[]{:T(128)}) all-reduce(f32[]{:T(128)S(6)} %add.124, f32[]{:T(128)} %get-tuple-element.18), channel_id=1, replica_groups=mesh['layer'=4,'row'=2,'col'=4] {'layer','row','col'}, use_global_device_ids=true, to_apply=%region_7.8 | all-reduce | flops 2 | bytes 16 | tf_op jit(solution)/shard_map/psum | solution.py:115
  193.4 3.9 %multiply_reduce_fusion = (f32[]{:T(128)}, f32[2,512,128]{2,1,0:T(8,128)S(1)}, f32[2,512,128]{2,1,0:T(8,128)}) fusion(f32[2,512,128]{2,1,0:T(8,128)} %get-tuple-element.61, f32[2,512,128]{2,1,0:T(8,128)S(1)} %copy-done.1, f32[2,512,128]{2,1,0:T(8,128)S(1)} %get-tuple-element.13, f32[1,512,128]{2,1,0:T(8,128)S(1)} %get-tuple-element.29, ...), kind=kOutput, calls=%fused_computation.134 | convolution fusion | flops 282915840 | bytes 5447688 | tf_op jit(solution)/shard_map/liq,qj->lij/dot_general | solution.py:53
  197.3 4.2 %collective-permute-start.25 = (f32[2,25,128]{2,1,0:T(8,128)S(1)}, f32[2,25,128]{2,1,0:T(8,128)S(1)}, u32[]{:S(2)}, u32[]{:S(2)}) collective-permute-start(f32[2,25,128]{2,1,0:T(8,128)S(1)} %get-tuple-element.26), channel_id=1, source_target_pairs={{0,4},{1,5},{2,6},{3,7},{8,12},{9,13},{10,14},{11,15},{16,20},{17,... | collective-permute-start | bytes 76808 | tf_op jit(solution)/shard_map/ppermute | solution.py:26
  203.1 4.2 %collective-permute-done.26 = f32[2,25,128]{2,1,0:T(8,128)S(1)} collective-permute-done((f32[2,25,128]{2,1,0:T(8,128)S(1)}, f32[2,25,128]{2,1,0:T(8,128)S(1)}, u32[]{:S(2)}, u32[]{:S(2)}) %collective-permute-start.26) | collective-permute-done | bytes 25632 | tf_op jit(solution)/shard_map/ppermute | solution.py:28
  212.4 2.9 %collective-permute-done.28 = f32[2,512,25]{1,2,0:T(8,128)S(1)} collective-permute-done((f32[2,512,25]{1,2,0:T(8,128)S(1)}, f32[2,512,25]{1,2,0:T(8,128)S(1)}, u32[]{:S(2)}, u32[]{:S(2)}) %collective-permute-start.28) | collective-permute-done | bytes 102432 | tf_op jit(solution)/shard_map/ppermute | solution.py:28
  215.3 2.5 multiply_reduce_fusion.2
  222.5 43.0 %all-reduce = (f32[]{:T(128)}, f32[]{:T(128)}) all-reduce(f32[]{:T(128)S(6)} %add.133, f32[]{:T(128)} %get-tuple-element.16), channel_id=1, replica_groups=mesh['layer'=4,'row'=2,'col'=4] {'layer','row','col'}, use_global_device_ids=true, to_apply=%region_12.13 | all-reduce | flops 2 | bytes 16 | tf_op jit(solution)/shard_map/psum | solution.py:115
  (108 shorter events, 51.4 us)
Async XLA Ops:
  1.4 11.0 %collective-permute-start = (f32[2,25,128]{2,1,0:T(8,128)S(1)}, f32[2,25,128]{2,1,0:T(8,128)S(1)}, u32[]{:S(2)}, u32[]{:S(2)}) collective-permute-start(f32[2,25,128]{2,1,0:T(8,128)S(1)} %get-tuple-element.56), channel_id=1, source_target_pairs={{0,4},{1,5},{2,6},{3,7},{8,12},{9,13},{10,14},{11,15},{16,20},{17,... | collective-permute-start | bytes 76808 | tf_op jit(solution)/shard_map/ppermute | solution.py:26
  6.3 6.2 %collective-permute-start.1 = (f32[2,25,128]{2,1,0:T(8,128)S(1)}, f32[2,25,128]{2,1,0:T(8,128)S(1)}, u32[]{:S(2)}, u32[]{:S(2)}) collective-permute-start(f32[2,25,128]{2,1,0:T(8,128)S(1)} %get-tuple-element.57), channel_id=1, source_target_pairs={{4,0},{5,1},{6,2},{7,3},{12,8},{13,9},{14,10},{15,11},{20,16},{21,... | collective-permute-start | bytes 76808 | tf_op jit(solution)/shard_map/ppermute | solution.py:28
  8.8 11.1 %collective-permute-start.4 = (f32[1,512,128]{2,1,0:T(8,128)S(1)}, f32[1,512,128]{2,1,0:T(8,128)S(1)}, u32[]{:S(2)}, u32[]{:S(2)}) collective-permute-start(f32[1,512,128]{2,1,0:T(8,128)S(1)} %get-tuple-element.52), channel_id=1, source_target_pairs={{0,8},{8,16},{16,24},{1,9},{9,17},{17,25},{2,10},{10,18},{18,26},{... | collective-permute-start | bytes 786440 | tf_op jit(solution)/shard_map/ppermute | solution.py:38
  14.9 5.0 %collective-permute-start.3 = (f32[2,512,25]{1,2,0:T(8,128)S(1)}, f32[2,512,25]{1,2,0:T(8,128)S(1)}, u32[]{:S(2)}, u32[]{:S(2)}) collective-permute-start(f32[2,512,25]{1,2,0:T(8,128)S(1)} %get-tuple-element.55), channel_id=1, source_target_pairs={{1,0},{2,1},{3,2},{5,4},{6,5},{7,6},{9,8},{10,9},{11,10},{13,12},{... | collective-permute-start | bytes 307208 | tf_op jit(solution)/shard_map/ppermute | solution.py:28
  22.5 6.1 %collective-permute-start.5 = (f32[2,25,128]{2,1,0:T(8,128)S(1)}, f32[2,25,128]{2,1,0:T(8,128)S(1)}, u32[]{:S(2)}, u32[]{:S(2)}) collective-permute-start(f32[2,25,128]{2,1,0:T(8,128)S(1)} %get-tuple-element.50), channel_id=1, source_target_pairs={{0,4},{1,5},{2,6},{3,7},{8,12},{9,13},{10,14},{11,15},{16,20},{17,... | collective-permute-start | bytes 76808 | tf_op jit(solution)/shard_map/ppermute | solution.py:26
  27.0 5.8 %collective-permute-start.6 = (f32[2,25,128]{2,1,0:T(8,128)S(1)}, f32[2,25,128]{2,1,0:T(8,128)S(1)}, u32[]{:S(2)}, u32[]{:S(2)}) collective-permute-start(f32[2,25,128]{2,1,0:T(8,128)S(1)} %get-tuple-element.51), channel_id=1, source_target_pairs={{4,0},{5,1},{6,2},{7,3},{12,8},{13,9},{14,10},{15,11},{20,16},{21,... | collective-permute-start | bytes 76808 | tf_op jit(solution)/shard_map/ppermute | solution.py:28
  33.8 6.7 %collective-permute-start.7 = (f32[2,512,25]{1,2,0:T(8,128)S(1)}, f32[2,512,25]{1,2,0:T(8,128)S(1)}, u32[]{:S(2)}, u32[]{:S(2)}) collective-permute-start(f32[2,512,25]{1,2,0:T(8,128)S(1)} %get-tuple-element.48), channel_id=1, source_target_pairs={{0,1},{1,2},{2,3},{4,5},{5,6},{6,7},{8,9},{9,10},{10,11},{12,13},{... | collective-permute-start | bytes 307208 | tf_op jit(solution)/shard_map/ppermute | solution.py:26
  39.2 12.8 %collective-permute-start.9 = (f32[1,512,128]{2,1,0:T(8,128)S(1)}, f32[1,512,128]{2,1,0:T(8,128)S(1)}, u32[]{:S(2)}, u32[]{:S(2)}) collective-permute-start(f32[1,512,128]{2,1,0:T(8,128)S(1)} %get-tuple-element.43), channel_id=1, source_target_pairs={{8,0},{16,8},{24,16},{9,1},{17,9},{25,17},{10,2},{18,10},{26,18},{... | collective-permute-start | bytes 786440 | tf_op jit(solution)/shard_map/ppermute | solution.py:38
  45.2 5.8 %collective-permute-start.11 = (f32[2,25,128]{2,1,0:T(8,128)S(1)}, f32[2,25,128]{2,1,0:T(8,128)S(1)}, u32[]{:S(2)}, u32[]{:S(2)}) collective-permute-start(f32[2,25,128]{2,1,0:T(8,128)S(1)} %get-tuple-element.47), channel_id=1, source_target_pairs={{4,0},{5,1},{6,2},{7,3},{12,8},{13,9},{14,10},{15,11},{20,16},{21,... | collective-permute-start | bytes 76808 | tf_op jit(solution)/shard_map/ppermute | solution.py:28
  52.9 53.5 %collective-permute-start.14 = (f32[1,512,128]{2,1,0:T(8,128)S(1)}, f32[1,512,128]{2,1,0:T(8,128)S(1)}, u32[]{:S(2)}, u32[]{:S(2)}) collective-permute-start(f32[1,512,128]{2,1,0:T(8,128)S(1)} %get-tuple-element.40), channel_id=1, source_target_pairs={{0,8},{8,16},{16,24},{1,9},{9,17},{17,25},{2,10},{10,18},{18,26},{... | collective-permute-start | bytes 786440 | tf_op jit(solution)/shard_map/ppermute | solution.py:38
  57.2 49.2 %collective-permute-start.12 = (f32[2,512,25]{1,2,0:T(8,128)}, f32[2,512,25]{1,2,0:T(8,128)}, u32[]{:S(2)}, u32[]{:S(2)}) collective-permute-start(f32[2,512,25]{1,2,0:T(8,128)} %get-tuple-element.44), channel_id=1, source_target_pairs={{0,1},{1,2},{2,3},{4,5},{5,6},{6,7},{8,9},{9,10},{10,11},{12,13},{... | collective-permute-start | bytes 307208 | tf_op jit(solution)/shard_map/ppermute | solution.py:26
  61.9 44.6 %collective-permute-start.13 = (f32[2,512,25]{1,2,0:T(8,128)}, f32[2,512,25]{1,2,0:T(8,128)}, u32[]{:S(2)}, u32[]{:S(2)}) collective-permute-start(f32[2,512,25]{1,2,0:T(8,128)} %get-tuple-element.45), channel_id=1, source_target_pairs={{1,0},{2,1},{3,2},{5,4},{6,5},{7,6},{9,8},{10,9},{11,10},{13,12},{... | collective-permute-start | bytes 307208 | tf_op jit(solution)/shard_map/ppermute | solution.py:28
  111.1 5.8 %collective-permute-start.15 = (f32[2,25,128]{2,1,0:T(8,128)S(1)}, f32[2,25,128]{2,1,0:T(8,128)S(1)}, u32[]{:S(2)}, u32[]{:S(2)}) collective-permute-start(f32[2,25,128]{2,1,0:T(8,128)S(1)} %get-tuple-element.38), channel_id=1, source_target_pairs={{0,4},{1,5},{2,6},{3,7},{8,12},{9,13},{10,14},{11,15},{16,20},{17,... | collective-permute-start | bytes 76808 | tf_op jit(solution)/shard_map/ppermute | solution.py:26
  115.2 5.8 %collective-permute-start.16 = (f32[2,25,128]{2,1,0:T(8,128)S(1)}, f32[2,25,128]{2,1,0:T(8,128)S(1)}, u32[]{:S(2)}, u32[]{:S(2)}) collective-permute-start(f32[2,25,128]{2,1,0:T(8,128)S(1)} %get-tuple-element.39), channel_id=1, source_target_pairs={{4,0},{5,1},{6,2},{7,3},{12,8},{13,9},{14,10},{15,11},{20,16},{21,... | collective-permute-start | bytes 76808 | tf_op jit(solution)/shard_map/ppermute | solution.py:28
  123.3 5.7 %collective-permute-start.18 = (f32[2,512,25]{1,2,0:T(8,128)S(1)}, f32[2,512,25]{1,2,0:T(8,128)S(1)}, u32[]{:S(2)}, u32[]{:S(2)}) collective-permute-start(f32[2,512,25]{1,2,0:T(8,128)S(1)} %get-tuple-element.37), channel_id=1, source_target_pairs={{1,0},{2,1},{3,2},{5,4},{6,5},{7,6},{9,8},{10,9},{11,10},{13,12},{... | collective-permute-start | bytes 307208 | tf_op jit(solution)/shard_map/ppermute | solution.py:28
  124.8 14.4 %collective-permute-start.19 = (f32[1,512,128]{2,1,0:T(8,128)S(1)}, f32[1,512,128]{2,1,0:T(8,128)S(1)}, u32[]{:S(2)}, u32[]{:S(2)}) collective-permute-start(f32[1,512,128]{2,1,0:T(8,128)S(1)} %get-tuple-element.31), channel_id=1, source_target_pairs={{8,0},{16,8},{24,16},{9,1},{17,9},{25,17},{10,2},{18,10},{26,18},{... | collective-permute-start | bytes 786440 | tf_op jit(solution)/shard_map/ppermute | solution.py:38
  132.4 5.8 %collective-permute-start.21 = (f32[2,25,128]{2,1,0:T(8,128)S(1)}, f32[2,25,128]{2,1,0:T(8,128)S(1)}, u32[]{:S(2)}, u32[]{:S(2)}) collective-permute-start(f32[2,25,128]{2,1,0:T(8,128)S(1)} %get-tuple-element.35), channel_id=1, source_target_pairs={{4,0},{5,1},{6,2},{7,3},{12,8},{13,9},{14,10},{15,11},{20,16},{21,... | collective-permute-start | bytes 76808 | tf_op jit(solution)/shard_map/ppermute | solution.py:28
  140.2 52.5 %collective-permute-start.24 = (f32[1,512,128]{2,1,0:T(8,128)S(1)}, f32[1,512,128]{2,1,0:T(8,128)S(1)}, u32[]{:S(2)}, u32[]{:S(2)}) collective-permute-start(f32[1,512,128]{2,1,0:T(8,128)S(1)} %get-tuple-element.28), channel_id=1, source_target_pairs={{0,8},{8,16},{16,24},{1,9},{9,17},{17,25},{2,10},{10,18},{18,26},{... | collective-permute-start | bytes 786440 | tf_op jit(solution)/shard_map/ppermute | solution.py:38
  143.3 49.4 %collective-permute-start.22 = (f32[2,512,25]{1,2,0:T(8,128)}, f32[2,512,25]{1,2,0:T(8,128)}, u32[]{:S(2)}, u32[]{:S(2)}) collective-permute-start(f32[2,512,25]{1,2,0:T(8,128)} %get-tuple-element.32), channel_id=1, source_target_pairs={{0,1},{1,2},{2,3},{4,5},{5,6},{6,7},{8,9},{9,10},{10,11},{12,13},{... | collective-permute-start | bytes 307208 | tf_op jit(solution)/shard_map/ppermute | solution.py:26
  148.0 44.7 %collective-permute-start.23 = (f32[2,512,25]{1,2,0:T(8,128)}, f32[2,512,25]{1,2,0:T(8,128)}, u32[]{:S(2)}, u32[]{:S(2)}) collective-permute-start(f32[2,512,25]{1,2,0:T(8,128)} %get-tuple-element.33), channel_id=1, source_target_pairs={{1,0},{2,1},{3,2},{5,4},{6,5},{7,6},{9,8},{10,9},{11,10},{13,12},{... | collective-permute-start | bytes 307208 | tf_op jit(solution)/shard_map/ppermute | solution.py:28
  197.3 5.8 %collective-permute-start.25 = (f32[2,25,128]{2,1,0:T(8,128)S(1)}, f32[2,25,128]{2,1,0:T(8,128)S(1)}, u32[]{:S(2)}, u32[]{:S(2)}) collective-permute-start(f32[2,25,128]{2,1,0:T(8,128)S(1)} %get-tuple-element.26), channel_id=1, source_target_pairs={{0,4},{1,5},{2,6},{3,7},{8,12},{9,13},{10,14},{11,15},{16,20},{17,... | collective-permute-start | bytes 76808 | tf_op jit(solution)/shard_map/ppermute | solution.py:26
  201.5 5.8 %collective-permute-start.26 = (f32[2,25,128]{2,1,0:T(8,128)S(1)}, f32[2,25,128]{2,1,0:T(8,128)S(1)}, u32[]{:S(2)}, u32[]{:S(2)}) collective-permute-start(f32[2,25,128]{2,1,0:T(8,128)S(1)} %get-tuple-element.27), channel_id=1, source_target_pairs={{4,0},{5,1},{6,2},{7,3},{12,8},{13,9},{14,10},{15,11},{20,16},{21,... | collective-permute-start | bytes 76808 | tf_op jit(solution)/shard_map/ppermute | solution.py:28
  209.5 5.7 %collective-permute-start.28 = (f32[2,512,25]{1,2,0:T(8,128)S(1)}, f32[2,512,25]{1,2,0:T(8,128)S(1)}, u32[]{:S(2)}, u32[]{:S(2)}) collective-permute-start(f32[2,512,25]{1,2,0:T(8,128)S(1)} %get-tuple-element.25), channel_id=1, source_target_pairs={{1,0},{2,1},{3,2},{5,4},{6,5},{7,6},{9,8},{10,9},{11,10},{13,12},{... | collective-permute-start | bytes 307208 | tf_op jit(solution)/shard_map/ppermute | solution.py:28
  211.0 8.6 %collective-permute-start.29 = (f32[1,512,128]{2,1,0:T(8,128)S(1)}, f32[1,512,128]{2,1,0:T(8,128)S(1)}, u32[]{:S(2)}, u32[]{:S(2)}) collective-permute-start(f32[1,512,128]{2,1,0:T(8,128)S(1)} %get-tuple-element.23), channel_id=1, source_target_pairs={{8,0},{16,8},{24,16},{9,1},{17,9},{25,17},{10,2},{18,10},{26,18},{... | collective-permute-start | bytes 786440 | tf_op jit(solution)/shard_map/ppermute | solution.py:38
  (22 other events, 157.5 us)
where the time goes:
time: 269 us; the launch traced here: 268 us
  blocking collectives  124 us (46%)
  starting transfers between devices  67.7 us (25%)
  waiting for transfers between devices  35 us (13%)
  matrix products  21.7 us (8%)
  between operations  10.6 us (4%)
  other arithmetic  4.76 us (2%)
  local copies, waits for them, and re-layouts  4.08 us (2%)
    psum x3, blocking collectives, local(): lax.psum((primal_sum, dual_sum), ('layer', 'row', 'col'))  124 us
    ppermute x12, starting transfers between devices, extended(): lax.ppermute(tail, axis, [(i, (i + 1) % count) for i in range(ends)])  38.4 us
    ppermute x12, waiting for transfers between devices, extended(): lax.ppermute(head, axis, [((i + 1) % count, i) for i in range(ends)])  32.1 us
    dot_general x6, matrix products, cols_pass(): jnp.einsum('liq,qj->lij', partial_sum, col_band, precision=lax.Precision....  16.3 us
    ppermute x12, starting transfers between devices, extended(): lax.ppermute(head, axis, [((i + 1) % count, i) for i in range(ends)])  15.9 us
    ppermute x6, starting transfers between devices, from_behind(): return lax.ppermute(block, axis, route)  13.4 us
    dot_general x6, matrix products, rows_pass(): jnp.einsum('ip,lpq->liq', row_band, padded, precision=lax.Precision.HIGHEST)  5.39 us
  transfers between devices with their start and end apart: 30, of which 15 were waited for; matrix products, arithmetic and copies ran while one was open for 4% of the time, Pallas kernels for 0%

commit v1 on v0

v1 whole, which is shorter than its diff:
```python
import functools

import jax
import jax.numpy as jnp
from jax import lax
from jax.experimental import pallas as pl
from jax.experimental.pallas import tpu as pltpu
from jax.sharding import PartitionSpec as P

WIN = 50
CAP_LEVELS = 8
ITERS = 3

step_eta = 0.4
low_density = 0.35
high_density = 0.65
layer_gap = 0.15
tiny_term = 1e-06

HALF = WIN // 2
HALO = -(-HALF // 16) * 16
TILE = 128
MESH = pl.DeviceIdType.MESH
DIRS = ((-1, 0), (1, 0), (0, -1), (0, 1), (-1, -1), (-1, 1), (1, -1), (1, 1))
F32 = jnp.float32
BF16 = jnp.bfloat16
NT = (((1,), (1,)), ((), ()))
NN = (((1,), (0,)), ((), ()))


def split(value):
    high = value.astype(BF16)
    low = (value - high.astype(F32)).astype(BF16)
    return high, low


def dot(left, right, dims=NN):
    return lax.dot_general(left, right, dims, preferred_element_type=F32)


def iota(shape, dim):
    return lax.broadcasted_iota(jnp.int32, shape, dim)


def window(offset, start):
    return jnp.where((offset >= start) & (offset < start + WIN), 1.0, 0.0).astype(BF16)


def kernel(
    sizes, cost, dens, capc, blocked, x_in, y_in, z_in,
    x, y_out, z, weight_out,
    ext_u, ext_y, et_u, et_y, ht_u, ht_y, above, below, zlow, cap, grad,
    band_r, band_h, band_c, band_d, pick, slots,
    send_sem, recv_sem, zsend, zrecv, ssend, srecv,
):
    nl, nr, nc = sizes
    layers, rows, cols = x_in.shape
    ndev = nl * nr * nc
    il, ir, ic = lax.axis_index("layer"), lax.axis_index("row"), lax.axis_index("col")
    me = (il * nr + ir) * nc + ic
    tiles = rows // TILE
    inverse_area = 1.0 / (WIN * WIN)
    own = pl.ds(HALO, rows)

    for ref in (ext_u, ext_y):
        ref[:, :HALO, :] = jnp.zeros((layers, HALO, cols), F32)
        ref[:, HALO + rows :, :] = jnp.zeros((layers, HALO, cols), F32)
    for ref in (ht_u, ht_y, above, below, zlow):
        ref[...] = jnp.zeros(ref.shape, F32)

    barrier = pltpu.get_barrier_semaphore()

    def greet(i, _):
        @pl.when(i != me)
        def _():
            pl.semaphore_signal(
                barrier, inc=1, device_id=(i // (nr * nc), (i // nc) % nr, i % nc),
                device_id_type=MESH,
            )
        return 0

    lax.fori_loop(0, ndev, greet, 0)

    keep_top = jnp.where(il < nl - 1, 1.0, 0.0).astype(F32)
    keep_low = jnp.where(il > 0, 1.0, 0.0).astype(F32)
    for which, start in ((0, -HALF), (1, 1 - HALF)):
        shape = (TILE, TILE + 2 * HALO)
        band_r[which] = window(iota(shape, 1) - HALO - iota(shape, 0), start)
        shape = (TILE, 3 * TILE)
        band_h[which] = window(iota(shape, 1) - TILE - iota(shape, 0), start)
        shape = (cols, cols)
        band_c[which] = window(iota(shape, 0) - iota(shape, 1), start)
        shape = (2 * HALO, cols)
        k = iota(shape, 0)
        place = jnp.where(k < HALO, k - HALO, k - HALO + cols)
        band_d[which] = window(place - iota(shape, 1), start)
    shape = (2 * HALO, cols)
    k = iota(shape, 0)
    place = jnp.where(k < HALO, k, k - 2 * HALO + cols)
    pick[...] = jnp.where(place == iota(shape, 1), 1.0, 0.0).astype(BF16)

    def span(t, base=0):
        return pl.ds(pl.multiple_of(t * TILE + base, 16), TILE)

    def lanes(t):
        return pl.ds(pl.multiple_of(t * TILE, TILE), TILE)

    def put_edges(et, l, t, value):
        high, low = split(value)
        et[l, :, lanes(t)] = dot(pick[...], high, NT) + dot(pick[...], low, NT)

    def prepare(t, _):
        for l in range(layers):
            value = y_in[l, span(t), :]
            ext_y[l, span(t, HALO), :] = value
            put_edges(et_y, l, t, value)
        return 0

    lax.fori_loop(0, tiles, prepare, 0)

    pl.semaphore_wait(barrier, ndev - 1)

    def copies(field):
        ext, et, ht = ((ext_u, et_u, ht_u), (ext_y, et_y, ht_y))[field]
        result = []
        for d, (dr, dc) in enumerate(DIRS):
            if dc == 0:
                src = ext.at[:, pl.ds(HALO if dr < 0 else rows, HALO), :]
                dst = ext.at[:, pl.ds(HALO + rows if dr < 0 else 0, HALO), :]
            else:
                from_rows = pl.ds(0 if dc < 0 else HALO, HALO)
                to_rows = pl.ds(HALO if dc < 0 else 0, HALO)
                if dr == 0:
                    src, dst = et.at[:, from_rows, :], ht.at[:, to_rows, pl.ds(TILE, rows)]
                elif dr < 0:
                    src = et.at[:, from_rows, pl.ds(0, TILE)]
                    dst = ht.at[:, to_rows, pl.ds(TILE + rows, TILE)]
                else:
                    src = et.at[:, from_rows, pl.ds(rows - TILE, TILE)]
                    dst = ht.at[:, to_rows, pl.ds(0, TILE)]
            to, frm = [], []
            if dr < 0:
                to.append(ir > 0)
                frm.append(ir < nr - 1)
            if dr > 0:
                to.append(ir < nr - 1)
                frm.append(ir > 0)
            if dc < 0:
                to.append(ic > 0)
                frm.append(ic < nc - 1)
            if dc > 0:
                to.append(ic < nc - 1)
                frm.append(ic > 0)
            copy = pltpu.make_async_remote_copy(
                src_ref=src, dst_ref=dst, send_sem=send_sem.at[field, d],
                recv_sem=recv_sem.at[field, d],
                device_id=(il, ir + dr, ic + dc), device_id_type=MESH,
            )
            result.append(
                (copy, functools.reduce(jnp.logical_and, to), functools.reduce(jnp.logical_and, frm))
            )
        return result

    halo_copies = (copies(0), copies(1))

    def begin(field, which):
        for d in which:
            copy, to, _ = halo_copies[field][d]
            pl.when(to)(copy.start)

    def finish(field):
        for copy, to, frm in halo_copies[field]:
            pl.when(frm)(copy.wait_recv)
            pl.when(to)(copy.wait_send)

    def up(src, dst, which=0):
        return pltpu.make_async_remote_copy(
            src_ref=src, dst_ref=dst, send_sem=zsend.at[which], recv_sem=zrecv.at[which],
            device_id=(il + 1, ir, ic), device_id_type=MESH,
        )

    def down(src, dst):
        return pltpu.make_async_remote_copy(
            src_ref=src, dst_ref=dst, send_sem=zsend.at[1], recv_sem=zrecv.at[1],
            device_id=(il - 1, ir, ic), device_id_type=MESH,
        )

    has_above, has_below = il < nl - 1, il > 0
    begin(1, (4, 5, 6, 7, 2, 3, 0, 1))
    first_up = up(z_in.at[layers - 1], zlow, 2)
    pl.when(has_above)(first_up.start)

    def begin_state(t, _):
        for l in range(layers):
            at = (l, span(t), slice(None))
            x[at] = x_in[at]
            z[at] = z_in[at] * keep_top if l == layers - 1 else z_in[at]
            level = (capc[at] + 1).astype(F32) * (1.0 / CAP_LEVELS)
            cap[at] = jnp.where(blocked[at] == 1, 0.0, level)
        return 0

    lax.fori_loop(0, tiles, begin_state, 0)

    def box(ext, ht, which, l, t):
        tall = pl.ds(pl.multiple_of(t * TILE, TILE), TILE + 2 * HALO)
        high, low = split(ext[l, tall, :])
        band = band_r[which]
        mid = dot(band, high) + dot(band, low)
        high, low = split(ht[l, :, pl.ds(pl.multiple_of(t * TILE, TILE), 3 * TILE)])
        band = band_h[which]
        side = dot(band, high, NT) + dot(band, low, NT)
        mid_high, mid_low = split(mid)
        side_high, side_low = split(side)
        return (
            dot(mid_high, band_c[which]) + dot(mid_low, band_c[which])
            + dot(side_high, band_d[which]) + dot(side_low, band_d[which])
        )

    def fold(value):
        return jnp.sum((value * value).reshape(TILE // 8, 8, cols), axis=0)

    none = jnp.zeros((8, cols), F32)
    weight = jnp.ones((1, cols), F32)
    for step in range(ITERS):
        last = step == ITERS - 1
        finish(1)

        def gradient(t, _):
            for l in range(layers):
                at = (l, span(t), slice(None))
                grad[at] = cost[at] + box(ext_y, ht_y, 1, l, t) * inverse_area
            return 0

        lax.fori_loop(0, tiles, gradient, 0)
        if step == 0:
            pl.when(has_below)(first_up.wait_recv)
            pl.when(has_above)(first_up.wait_send)
        else:
            sums_done()
            both = jnp.sum(slots[step - 1], axis=0)
            primal = jnp.sum(both[0:1], axis=1, keepdims=True)
            dual = jnp.sum(both[1:2], axis=1, keepdims=True)
            ratio = jnp.broadcast_to((dual + tiny_term) / (primal + tiny_term), (1, cols))
            weight = jnp.sqrt(weight) * jnp.sqrt(jnp.sqrt(ratio))
        tau = step_eta / weight
        sigma = step_eta * weight
        sigma_inverse = 1.0 / sigma

        def primal_move(t, total):
            for l in range(layers):
                at = (l, span(t), slice(None))
                earlier = zlow[span(t), :] if l == 0 else z[l - 1, span(t), :]
                old = x[at]
                new = jnp.minimum(
                    jnp.maximum(old - tau * (grad[at] + (z[at] - earlier)), 0.0), cap[at]
                )
                moved = new - old
                x[at] = new
                total = total + fold(moved)
                value = new + moved + dens[at]
                ext_u[l, span(t, HALO), :] = value
                put_edges(et_u, l, t, value)
            return total

        primal_sum = lax.fori_loop(0, tiles, primal_move, none)
        begin(0, (4, 5, 6, 7, 2, 3, 0, 1))
        send_down = down(ext_u.at[0, own, :], above)
        if not last:
            send_up = up(ext_u.at[layers - 1, own, :], below)
            pl.when(has_above)(send_up.start)
        pl.when(has_below)(send_down.start)
        finish(0)

        def dual_move(t, total):
            for l in range(layers):
                at = (l, span(t), slice(None))
                old = ext_y[l, span(t, HALO), :]
                term = old * sigma_inverse + box(ext_u, ht_u, 0, l, t) * inverse_area
                capped = jnp.minimum(term, high_density)
                clipped = jnp.where(
                    blocked[at] == 0, jnp.maximum(capped, low_density), capped
                )
                new = sigma * (term - clipped)
                total = total + fold(new - old)
                if last:
                    y_out[at] = new
                else:
                    ext_y[l, span(t, HALO), :] = new
                    put_edges(et_y, l, t, new)
            return total

        dual_sum = lax.fori_loop(0, tiles, dual_move, none)
        if not last:
            begin(1, (4, 5, 6, 7, 2, 3, 0, 1))

        pl.when(has_above)(send_down.wait_recv)
        pl.when(has_below)(send_down.wait_send)
        if not last:
            pl.when(has_below)(send_up.wait_recv)
            pl.when(has_above)(send_up.wait_send)

        def layer_move(t, total):
            def update(old, here, later, keep):
                term = old * sigma_inverse + keep * (here - later)
                return sigma * (term - jnp.clip(term, -layer_gap, layer_gap)) * keep

            levels = [ext_u[l, span(t, HALO), :] for l in range(layers)] + [above[span(t), :]]
            for l in range(layers):
                at = (l, span(t), slice(None))
                old = z[at]
                new = update(old, levels[l], levels[l + 1], keep_top if l == layers - 1 else 1.0)
                z[at] = new
                total = total + fold(new - old)
            if not last:
                zlow[span(t), :] = update(zlow[span(t), :], below[span(t), :], levels[0], keep_low)
            return total

        dual_sum = lax.fori_loop(0, tiles, layer_move, dual_sum)
        slots[step, pl.ds(me, 1)] = jnp.concatenate(
            [jnp.sum(primal_sum, axis=0, keepdims=True), jnp.sum(dual_sum, axis=0, keepdims=True)],
            axis=0,
        )[None]

        def tell(i, _, step=step):
            @pl.when(i != me)
            def _():
                pltpu.make_async_remote_copy(
                    src_ref=slots.at[step, me], dst_ref=slots.at[step, me],
                    send_sem=ssend.at[step], recv_sem=srecv.at[step],
                    device_id=(i // (nr * nc), (i // nc) % nr, i % nc), device_id_type=MESH,
                ).start()
            return 0

        lax.fori_loop(0, ndev, tell, 0)

        def sums_done(step=step):
            some = slots.at[step, pl.ds(0, ndev - 1)]
            pltpu.make_async_copy(some, some, srecv.at[step]).wait()
            pltpu.make_async_copy(some, some, ssend.at[step]).wait()

    sums_done()
    both = jnp.sum(slots[ITERS - 1], axis=0)
    primal = jnp.sum(both[0:1], axis=1, keepdims=True)
    dual = jnp.sum(both[1:2], axis=1, keepdims=True)
    ratio = jnp.broadcast_to((dual + tiny_term) / (primal + tiny_term), (1, cols))
    weight_out[...] = jnp.sqrt(weight) * jnp.sqrt(jnp.sqrt(ratio))


def local(sizes, *args):
    layers, rows, cols = args[0].shape
    ndev = sizes[0] * sizes[1] * sizes[2]
    whole = jax.ShapeDtypeStruct((layers, rows, cols), F32)
    vmem = pl.BlockSpec(memory_space=pltpu.VMEM)
    ext = pltpu.VMEM((layers, rows + 2 * HALO, cols), F32)
    et = pltpu.VMEM((layers, 2 * HALO, rows), F32)
    ht = pltpu.VMEM((layers, 2 * HALO, rows + 2 * TILE), F32)
    plane = pltpu.VMEM((rows, cols), F32)
    full = pltpu.VMEM((layers, rows, cols), F32)
    x, y, z, weight = pl.pallas_call(
        functools.partial(kernel, sizes),
        out_shape=(whole, whole, whole, jax.ShapeDtypeStruct((1, cols), F32)),
        in_specs=[vmem] * 7,
        out_specs=(vmem,) * 4,
        scratch_shapes=[
            ext, ext, et, et, ht, ht, plane, plane, plane, full, full,
            pltpu.VMEM((2, TILE, TILE + 2 * HALO), BF16),
            pltpu.VMEM((2, TILE, 3 * TILE), BF16),
            pltpu.VMEM((2, cols, cols), BF16),
            pltpu.VMEM((2, 2 * HALO, cols), BF16),
            pltpu.VMEM((2 * HALO, cols), BF16),
            pltpu.VMEM((ITERS, ndev, 2, cols), F32),
            pltpu.SemaphoreType.DMA((2, 8)),
            pltpu.SemaphoreType.DMA((2, 8)),
            pltpu.SemaphoreType.DMA((3,)),
            pltpu.SemaphoreType.DMA((3,)),
            pltpu.SemaphoreType.DMA((ITERS,)),
            pltpu.SemaphoreType.DMA((ITERS,)),
        ],
        compiler_params=pltpu.CompilerParams(collective_id=0, has_side_effects=True),
        name="fill_steps",
    )(*args)
    return x, y, z, weight[0, 0]


def solution(mesh):
    sizes = tuple(mesh.shape[axis] for axis in ("layer", "row", "col"))
    spec = P("layer", "row", "col")
    return jax.shard_map(
        functools.partial(local, sizes),
        mesh=mesh,
        in_specs=(spec,) * 7,
        out_specs=(spec, spec, spec, P()),
        check_vma=False,
    )
```

time: 269 us -> 67.1 us (0.25)
  blocking collectives: 124 us -> 0 us
  starting transfers between devices: 67.7 us -> 0 us
  Pallas kernels: 0 us -> 61.1 us
  waiting for transfers between devices: 35 us -> 0 us
  matrix products: 21.7 us -> 0 us
  between operations: 10.6 us -> 1.82 us
  other arithmetic: 4.76 us -> 0 us
    psum x3 -> x0, blocking collectives: 124 us -> none  [local(): lax.psum((primal_sum, dual_sum), ('layer', 'row', 'col'))]
    ppermute x30 -> x0, starting transfers between devices: 67.7 us -> none  [the longest x12 38.4 us: extended(): lax.ppermute(tail, axis, [(i, (i + 1) % count) for i in range(ends)])]
    pallas_call x0 -> x1, Pallas kernels: none -> 61.1 us  [local(): pl.pallas_call(functools.partial(kernel, sizes), out_shape=(whole, whole,...]
    ppermute x30 -> x0, waiting for transfers between devices: 35 us -> none  [the longest x12 32.1 us: extended(): lax.ppermute(head, axis, [((i + 1) % count, i) for i in range(ends)])]
    dot_general x12 -> x0, matrix products: 21.7 us -> none  [the longest x6 16.3 us: cols_pass(): jnp.einsum('liq,qj->lij', partial_sum, col_band, precision=lax.Precision....]
    reduce_sum x3 -> x0, other arithmetic: 3.54 us -> none  [local(): jnp.sum(stacked_move * stacked_move)]
  transfers between devices with their start and end apart: 30 -> 0, of which waited for: 15 -> 0; matrix products, arithmetic and copies ran while one was open for 4% -> 0% of each run, Pallas kernels for 0% -> 0%
where the time goes in v1:
time: 67.1 us; the launch traced here: 66.9 us
  Pallas kernels  61.1 us (91%)
  local copies, waits for them, and re-layouts  3.96 us (6%)
  between operations  1.82 us (3%)
    pallas_call x1, Pallas kernels, local(): pl.pallas_call(functools.partial(kernel, sizes), out_shape=(whole, whole,...  61.1 us
    unnamed x9, local copies, waits for them, and re-layouts  3.96 us

profile of v1, /device:TPU:0, one launch (start us, length us, event | category | flops | bytes accessed | tf_op | source)
XLA Modules:
  0.0 66.9 jit_solution(14082394168437235136)
XLA Ops:
  0.6 61.1 %fill_steps.1 = (f32[2,512,128]{2,1,0:T(8,128)}, f32[2,512,128]{2,1,0:T(8,128)}, f32[2,512,128]{2,1,0:T(8,128)}, f32[1,128]{1,0:T(1,128)}) custom-call(f32[2,512,128]{2,1,0:T(8,128)} %cost.1, f32[2,512,128]{2,1,0:T(8,128)} %dens.1, s32[2,512,128]{2,1,0:T(8,128)} %capc.1, s32[2,512,128]{2,1,0:T(8,128)} %blocked.1, f32[2,512,128]{2,1,0:T(8,128)} %x_in.1, ...), custom_call_target="tpu_custom_call" | custom-call | tf_op jit(solution)/shard_map/fill_steps/pallas_call | solution.py:359
  61.7 0.0 copy-start.1
  61.7 1.9 %copy.15 = f32[2,512,128]{2,1,0:T(8,128)} copy(f32[2,512,128]{2,1,0:T(8,128)} %get-tuple-element.16) | data formatting | bytes 1048576
  63.7 0.0 copy-done.1
  63.7 0.0 copy-start
  63.7 0.8 %copy.16 = f32[2,512,128]{2,1,0:T(8,128)} copy(f32[2,512,128]{2,1,0:T(8,128)S(1)} %copy-done.1) | data formatting | bytes 1048576
  64.5 0.4 copy-done
  64.9 0.0 copy-start.2
  64.9 0.8 %copy.17 = f32[2,512,128]{2,1,0:T(8,128)} copy(f32[2,512,128]{2,1,0:T(8,128)S(1)} %copy-done) | data formatting | bytes 1048576
  65.7 0.0 copy-done.2
Async XLA Ops:
  61.7 1.9 %copy-start.1 = (f32[2,512,128]{2,1,0:T(8,128)S(1)}, f32[2,512,128]{2,1,0:T(8,128)}, u32[]{:S(2)}) copy-start(f32[2,512,128]{2,1,0:T(8,128)} %get-tuple-element.17) | copy-start | bytes 1572868
  63.7 1.2 %copy-start = (f32[2,512,128]{2,1,0:T(8,128)S(1)}, f32[2,512,128]{2,1,0:T(8,128)}, u32[]{:S(2)}) copy-start(f32[2,512,128]{2,1,0:T(8,128)} %get-tuple-element.18) | copy-start | bytes 1572868
  64.9 0.8 %copy-start.2 = (f32[1,128]{1,0:T(1,128)S(1)}, f32[1,128]{1,0:T(1,128)}, u32[]{:S(2)}) copy-start(f32[1,128]{1,0:T(1,128)} %get-tuple-element.11) | copy-start | bytes 1540

commit v2 on v1

v2 whole, which is shorter than its diff:
```python
import functools

import jax
import jax.numpy as jnp
from jax import lax
from jax.experimental import pallas as pl
from jax.experimental.pallas import tpu as pltpu
from jax.sharding import PartitionSpec as P

WIN = 50
CAP_LEVELS = 8
ITERS = 3

step_eta = 0.4
low_density = 0.35
high_density = 0.65
layer_gap = 0.15
tiny_term = 1e-06

HALF = WIN // 2
HALO = -(-HALF // 16) * 16
TILE = 128
MESH = pl.DeviceIdType.MESH
DIRS = ((-1, 0), (1, 0), (0, -1), (0, 1), (-1, -1), (-1, 1), (1, -1), (1, 1))
F32 = jnp.float32
BF16 = jnp.bfloat16
NT = (((1,), (1,)), ((), ()))
NN = (((1,), (0,)), ((), ()))


def split(value):
    high = value.astype(BF16)
    low = (value - high.astype(F32)).astype(BF16)
    return high, low


def dot(left, right, dims=NN):
    return lax.dot_general(left, right, dims, preferred_element_type=F32)


def iota(shape, dim):
    return lax.broadcasted_iota(jnp.int32, shape, dim)


def window(offset, start):
    return jnp.where((offset >= start) & (offset < start + WIN), 1.0, 0.0).astype(BF16)


def kernel(
    sizes, cost_in, dens_in, capc_in, blocked_in, x_in, y_in, z_in,
    x, y_out, z, weight_out,
    cost, dens, capc, blocked,
    ext_u, ext_y, et_u, et_y, ht_u, ht_y, above, below, zlow, cap, grad,
    band_r, band_h, band_c, band_d, pick, plane_slots, layer_slots,
    load_sem, send_sem, recv_sem, first_sem, zsend, zrecv, sum_sem,
):
    nl, nr, nc = sizes
    layers, rows, cols = x_in.shape
    peers = nr * nc
    il, ir, ic = lax.axis_index("layer"), lax.axis_index("row"), lax.axis_index("col")
    me = ir * nc + ic
    tiles = rows // TILE
    order = list(dict.fromkeys((0, tiles - 1, *range(tiles))))
    inverse_area = 1.0 / (WIN * WIN)
    own = pl.ds(HALO, rows)

    pairs = (
        (y_in, ext_y.at[:, own, :]), (x_in, x), (z_in, z), (cost_in, cost), (capc_in, capc),
        (blocked_in, blocked), (dens_in, dens),
    )
    loads = [pltpu.make_async_copy(a, b, load_sem.at[n]) for n, (a, b) in enumerate(pairs)]
    for load in loads:
        load.start()

    for ref in (ext_u, ext_y):
        ref[:, :HALO, :] = jnp.zeros((layers, HALO, cols), F32)
        ref[:, HALO + rows :, :] = jnp.zeros((layers, HALO, cols), F32)
    for ref in (ht_u, ht_y, above, below, zlow):
        ref[...] = jnp.zeros(ref.shape, F32)

    barrier = pltpu.get_barrier_semaphore()

    def in_plane(act):
        def one(i, _):
            pl.when(i != me)(lambda: act((il, i // nc, i % nc)))
            return 0

        lax.fori_loop(0, peers, one, 0, unroll=peers <= 16)

    def in_stack(act):
        for i in range(nl):
            pl.when(i != il)(lambda i=i: act((i, ir, ic)))

    def greet(device):
        pl.semaphore_signal(barrier, inc=1, device_id=device, device_id_type=MESH)

    in_plane(greet)
    in_stack(greet)

    keep_top = jnp.where(il < nl - 1, 1.0, 0.0).astype(F32)
    keep_low = jnp.where(il > 0, 1.0, 0.0).astype(F32)
    for which, start in ((0, -HALF), (1, 1 - HALF)):
        shape = (TILE, TILE + 2 * HALO)
        band_r[which] = window(iota(shape, 1) - HALO - iota(shape, 0), start)
        shape = (TILE, 3 * TILE)
        band_h[which] = window(iota(shape, 1) - TILE - iota(shape, 0), start)
        shape = (cols, cols)
        band_c[which] = window(iota(shape, 0) - iota(shape, 1), start)
        shape = (2 * HALO, cols)
        k = iota(shape, 0)
        place = jnp.where(k < HALO, k - HALO, k - HALO + cols)
        band_d[which] = window(place - iota(shape, 1), start)
    shape = (2 * HALO, cols)
    k = iota(shape, 0)
    place = jnp.where(k < HALO, k, k - 2 * HALO + cols)
    pick[...] = jnp.where(place == iota(shape, 1), 1.0, 0.0).astype(BF16)

    def span(t, base=0):
        return pl.ds(t * TILE + base, TILE)

    def put_edges(et, l, t, value):
        high, low = split(value)
        et[l, :, span(t)] = dot(pick[...], high, NT) + dot(pick[...], low, NT)

    loads[0].wait()
    for t in range(tiles):
        for l in range(layers):
            put_edges(et_y, l, t, ext_y[l, span(t, HALO), :])

    pl.semaphore_wait(barrier, peers - 1 + nl - 1)

    def copies(field):
        ext, et, ht = ((ext_u, et_u, ht_u), (ext_y, et_y, ht_y))[field]
        result = []
        for d, (dr, dc) in enumerate(DIRS):
            if dc == 0:
                src = ext.at[:, pl.ds(HALO if dr < 0 else rows, HALO), :]
                dst = ext.at[:, pl.ds(HALO + rows if dr < 0 else 0, HALO), :]
            else:
                from_rows = pl.ds(0 if dc < 0 else HALO, HALO)
                to_rows = pl.ds(HALO if dc < 0 else 0, HALO)
                if dr == 0:
                    src, dst = et.at[:, from_rows, :], ht.at[:, to_rows, pl.ds(TILE, rows)]
                elif dr < 0:
                    src = et.at[:, from_rows, pl.ds(0, TILE)]
                    dst = ht.at[:, to_rows, pl.ds(TILE + rows, TILE)]
                else:
                    src = et.at[:, from_rows, pl.ds(rows - TILE, TILE)]
                    dst = ht.at[:, to_rows, pl.ds(0, TILE)]
            to, frm = [], []
            if dr < 0:
                to.append(ir > 0)
                frm.append(ir < nr - 1)
            if dr > 0:
                to.append(ir < nr - 1)
                frm.append(ir > 0)
            if dc < 0:
                to.append(ic > 0)
                frm.append(ic < nc - 1)
            if dc > 0:
                to.append(ic < nc - 1)
                frm.append(ic > 0)
            copy = pltpu.make_async_remote_copy(
                src_ref=src, dst_ref=dst, send_sem=send_sem.at[field, d],
                recv_sem=recv_sem.at[field, d],
                device_id=(il, ir + dr, ic + dc), device_id_type=MESH,
            )
            result.append(
                (copy, functools.reduce(jnp.logical_and, to), functools.reduce(jnp.logical_and, frm))
            )
        return result

    halo_copies = (copies(0), copies(1))

    def begin(field, which):
        for d in which:
            copy, to, _ = halo_copies[field][d]
            pl.when(to)(copy.start)

    def finish(field):
        for copy, to, frm in halo_copies[field]:
            pl.when(frm)(copy.wait_recv)
            pl.when(to)(copy.wait_send)

    has_above, has_below = il < nl - 1, il > 0
    EDGE, SIDE = (4, 5, 6, 7, 0, 1), (2, 3)
    begin(1, EDGE + SIDE)
    first_up = pltpu.make_async_remote_copy(
        src_ref=z_in.at[layers - 1], dst_ref=zlow, send_sem=first_sem.at[0],
        recv_sem=first_sem.at[1], device_id=(il + 1, ir, ic), device_id_type=MESH,
    )
    pl.when(has_above)(first_up.start)

    def up(t):
        return pltpu.make_async_remote_copy(
            src_ref=ext_u.at[layers - 1, span(t, HALO), :], dst_ref=below.at[span(t), :],
            send_sem=zsend.at[0, t], recv_sem=zrecv.at[0, t],
            device_id=(il + 1, ir, ic), device_id_type=MESH,
        )

    def down(t):
        return pltpu.make_async_remote_copy(
            src_ref=ext_u.at[0, span(t, HALO), :], dst_ref=above.at[span(t), :],
            send_sem=zsend.at[1, t], recv_sem=zrecv.at[1, t],
            device_id=(il - 1, ir, ic), device_id_type=MESH,
        )

    def inner(ext, which, l, t):
        first = HALO if t == 0 else 0
        end = TILE + HALO if t == tiles - 1 else TILE + 2 * HALO
        high, low = split(ext[l, t * TILE + first : t * TILE + end, :])
        band = band_r[which, :, first:end]
        high, low = split(dot(band, high) + dot(band, low))
        return dot(high, band_c[which]) + dot(low, band_c[which])

    def outer(ext, ht, which, l, t):
        high, low = split(ht[l, :, t * TILE : (t + 3) * TILE])
        band = band_h[which]
        high, low = split(dot(band, high, NT) + dot(band, low, NT))
        total = dot(high, band_d[which]) + dot(low, band_d[which])
        for edge, at, base in ((0, 0, 0), (tiles - 1, TILE + HALO, HALO + rows)):
            if t == edge:
                high, low = split(ext[l, base : base + HALO, :])
                band = band_r[which, :, at : at + HALO]
                high, low = split(dot(band, high) + dot(band, low))
                total = total + dot(high, band_c[which]) + dot(low, band_c[which])
        return total

    everywhere = [(l, t, (l, span(t), slice(None))) for t in order for l in range(layers)]
    for n in range(1, 7):
        loads[n].wait()
    z[layers - 1] = z[layers - 1] * keep_top
    for l, t, at in everywhere:
        level = (capc[at] + 1).astype(F32) * (1.0 / CAP_LEVELS)
        cap[at] = jnp.where(blocked[at] == 1, 0.0, level)

    def fold(value):
        return jnp.sum((value * value).reshape(TILE // 8, 8, cols), axis=0)

    def sum_copy(slots, step, mine, stage, device):
        return pltpu.make_async_remote_copy(
            src_ref=slots.at[step, mine], dst_ref=slots.at[step, mine],
            send_sem=sum_sem.at[stage, 0, step], recv_sem=sum_sem.at[stage, 1, step],
            device_id=device, device_id_type=MESH,
        )

    def sums_wait(slots, step, stage, count):
        if count > 1:
            some = slots.at[step, pl.ds(0, count - 1)]
            pltpu.make_async_copy(some, some, sum_sem.at[stage, 1, step]).wait()
            pltpu.make_async_copy(some, some, sum_sem.at[stage, 0, step]).wait()

    def sums_begin(step, primal_sum, dual_sum):
        plane_slots[step, pl.ds(me, 1)] = jnp.concatenate(
            [jnp.sum(primal_sum, axis=0, keepdims=True), jnp.sum(dual_sum, axis=0, keepdims=True)],
            axis=0,
        )[None]
        in_plane(lambda device: sum_copy(plane_slots, step, me, 0, device).start())

    def sums_forward(step):
        sums_wait(plane_slots, step, 0, peers)
        layer_slots[step, pl.ds(il, 1)] = jnp.sum(plane_slots[step], axis=0)[None]
        in_stack(lambda device: sum_copy(layer_slots, step, il, 1, device).start())

    def sums_end(step, weight):
        sums_wait(layer_slots, step, 1, nl)
        both = jnp.sum(layer_slots[step], axis=0)
        primal = jnp.sum(both[0:1], axis=1, keepdims=True)
        dual = jnp.sum(both[1:2], axis=1, keepdims=True)
        ratio = jnp.broadcast_to((dual + tiny_term) / (primal + tiny_term), (1, cols))
        return jnp.sqrt(weight) * jnp.sqrt(jnp.sqrt(ratio))

    weight = jnp.ones((1, cols), F32)
    for step in range(ITERS):
        last = step == ITERS - 1
        for l, t, at in everywhere:
            grad[at] = cost[at] + inner(ext_y, 1, l, t) * inverse_area
        if step > 0:
            sums_forward(step - 1)
        else:
            pl.when(has_below)(first_up.wait_recv)
            pl.when(has_above)(first_up.wait_send)
        finish(1)
        for l, t, at in everywhere:
            earlier = zlow[span(t), :] if l == 0 else z[l - 1, span(t), :]
            grad[at] = grad[at] + outer(ext_y, ht_y, 1, l, t) * inverse_area + (z[at] - earlier)
        if step > 0:
            weight = sums_end(step - 1, weight)
        tau = step_eta / weight
        sigma = step_eta * weight
        sigma_inverse = 1.0 / sigma

        primal_sum = jnp.zeros((8, cols), F32)
        for l, t, at in everywhere:
            old = x[at]
            new = jnp.minimum(jnp.maximum(old - tau * grad[at], 0.0), cap[at])
            moved = new - old
            x[at] = new
            primal_sum = primal_sum + fold(moved)
            value = new + moved + dens[at]
            ext_u[l, span(t, HALO), :] = value
            put_edges(et_u, l, t, value)
            if l == layers - 1:
                if not last:
                    pl.when(has_above)(up(t).start)
                pl.when(has_below)(down(t).start)
                if t == order[min(1, tiles - 1)]:
                    begin(0, EDGE)
        begin(0, SIDE)
        for l, t, at in everywhere:
            grad[at] = inner(ext_u, 0, l, t)
        finish(0)

        dual_sum = jnp.zeros((8, cols), F32)
        for l, t, at in everywhere:
            old = ext_y[l, span(t, HALO), :]
            term = old * sigma_inverse + (grad[at] + outer(ext_u, ht_u, 0, l, t)) * inverse_area
            capped = jnp.minimum(term, high_density)
            clipped = jnp.where(blocked[at] == 0, jnp.maximum(capped, low_density), capped)
            new = sigma * (term - clipped)
            dual_sum = dual_sum + fold(new - old)
            if last:
                y_out[at] = new
            else:
                ext_y[l, span(t, HALO), :] = new
                put_edges(et_y, l, t, new)
                if l == layers - 1 and t == order[min(1, tiles - 1)]:
                    begin(1, EDGE)
        if not last:
            begin(1, SIDE)

        def update(old, here, later, keep):
            term = old * sigma_inverse + keep * (here - later)
            return sigma * (term - jnp.clip(term, -layer_gap, layer_gap)) * keep

        for t in order:
            pl.when(has_above)(down(t).wait_recv)
            pl.when(has_below)(down(t).wait_send)
            if not last:
                pl.when(has_below)(up(t).wait_recv)
                pl.when(has_above)(up(t).wait_send)
            levels = [ext_u[l, span(t, HALO), :] for l in range(layers)] + [above[span(t), :]]
            for l in range(layers):
                at = (l, span(t), slice(None))
                old = z[at]
                new = update(old, levels[l], levels[l + 1], keep_top if l == layers - 1 else 1.0)
                z[at] = new
                dual_sum = dual_sum + fold(new - old)
            if not last:
                zlow[span(t), :] = update(zlow[span(t), :], below[span(t), :], levels[0], keep_low)
        sums_begin(step, primal_sum, dual_sum)

    sums_forward(ITERS - 1)
    weight_out[...] = sums_end(ITERS - 1, weight)


def local(sizes, *args):
    layers, rows, cols = args[0].shape
    peers = sizes[1] * sizes[2]
    tiles = rows // TILE
    whole = jax.ShapeDtypeStruct((layers, rows, cols), F32)
    vmem = pl.BlockSpec(memory_space=pltpu.VMEM)
    anywhere = pl.BlockSpec(memory_space=pl.ANY)
    full = pltpu.VMEM((layers, rows, cols), F32)
    full_int = pltpu.VMEM((layers, rows, cols), jnp.int32)
    line = pltpu.VMEM((1, cols), F32)
    ext = pltpu.VMEM((layers, rows + 2 * HALO, cols), F32)
    et = pltpu.VMEM((layers, 2 * HALO, rows), F32)
    ht = pltpu.VMEM((layers, 2 * HALO, rows + 2 * TILE), F32)
    plane = pltpu.VMEM((rows, cols), F32)
    x, y, z, weight = pl.pallas_call(
        functools.partial(kernel, sizes),
        out_shape=(full, full, full, line),
        in_specs=[anywhere] * 7,
        out_specs=(vmem,) * 4,
        scratch_shapes=[
            full, full, full_int, full_int,
            ext, ext, et, et, ht, ht, plane, plane, plane, full, full,
            pltpu.VMEM((2, TILE, TILE + 2 * HALO), BF16),
            pltpu.VMEM((2, TILE, 3 * TILE), BF16),
            pltpu.VMEM((2, cols, cols), BF16),
            pltpu.VMEM((2, 2 * HALO, cols), BF16),
            pltpu.VMEM((2 * HALO, cols), BF16),
            pltpu.VMEM((ITERS, peers, 2, cols), F32),
            pltpu.VMEM((ITERS, sizes[0], 2, cols), F32),
            pltpu.SemaphoreType.DMA((7,)),
            pltpu.SemaphoreType.DMA((2, 8)),
            pltpu.SemaphoreType.DMA((2, 8)),
            pltpu.SemaphoreType.DMA((2,)),
            pltpu.SemaphoreType.DMA((2, tiles)),
            pltpu.SemaphoreType.DMA((2, tiles)),
            pltpu.SemaphoreType.DMA((2, 2, ITERS)),
        ],
        compiler_params=pltpu.CompilerParams(collective_id=0, has_side_effects=True),
        name="fill_steps",
    )(*args)
    return x, y, z, weight[0, 0]


def solution(mesh):
    sizes = tuple(mesh.shape[axis] for axis in ("layer", "row", "col"))
    spec = P("layer", "row", "col")
    return jax.shard_map(
        functools.partial(local, sizes),
        mesh=mesh,
        in_specs=(spec,) * 7,
        out_specs=(spec, spec, spec, P()),
        check_vma=False,
    )
```

time: 67.1 us -> 64 us (0.954)
  local copies, waits for them, and re-layouts: 3.96 us -> 2.38 us
  Pallas kernels: 61.1 us -> 59.7 us
    unnamed x9 -> x3, local copies, waits for them, and re-layouts: 3.96 us -> 2.38 us
    pallas_call x1, Pallas kernels: 61.1 us -> 59.7 us  [local(): pl.pallas_call(functools.partial(kernel, sizes), out_shape=(full, full, f...]
where the time goes in v2:
time: 64 us; the launch traced here: 63.9 us
  Pallas kernels  59.7 us (93%)
  local copies, waits for them, and re-layouts  2.38 us (4%)
  between operations  1.81 us (3%)
    pallas_call x1, Pallas kernels, local(): pl.pallas_call(functools.partial(kernel, sizes), out_shape=(full, full, f...  59.7 us
    unnamed x3, local copies, waits for them, and re-layouts  2.38 us

profile of v2, /device:TPU:0, one launch (start us, length us, event | category | flops | bytes accessed | tf_op | source)
XLA Modules:
  0.0 63.9 jit_solution(17156184152924509831)
XLA Ops:
  0.6 59.7 %fill_steps.1 = (f32[2,512,128]{2,1,0:T(8,128)S(1)}, f32[2,512,128]{2,1,0:T(8,128)S(1)}, f32[2,512,128]{2,1,0:T(8,128)S(1)}, f32[1,128]{1,0:T(1,128)S(1)}) custom-call(f32[2,512,128]{2,1,0:T(8,128)} %cost_in.1, f32[2,512,128]{2,1,0:T(8,128)} %dens_in.1, s32[2,512,128]{2,1,0:T(8,128)} %capc_in.1, s32[2,512,128]{2,1,0:T(8,128)} %blocked_in.1, ...), custom_call_target="tpu_custom_call" | custom-call | tf_op jit(solution)/shard_map/fill_steps/pallas_call | solution.py:371
  60.3 0.8 %copy.15 = f32[2,512,128]{2,1,0:T(8,128)} copy(f32[2,512,128]{2,1,0:T(8,128)S(1)} %get-tuple-element.12) | data formatting | bytes 1048576
  61.1 0.8 %copy.16 = f32[2,512,128]{2,1,0:T(8,128)} copy(f32[2,512,128]{2,1,0:T(8,128)S(1)} %get-tuple-element.13) | data formatting | bytes 1048576
  61.9 0.8 %copy.17 = f32[2,512,128]{2,1,0:T(8,128)} copy(f32[2,512,128]{2,1,0:T(8,128)S(1)} %get-tuple-element.14) | data formatting | bytes 1048576

commit v3 on v2

--- a/solution.py
+++ b/solution.py
@@ -51,14 +51,14 @@
     x, y_out, z, weight_out,
     cost, dens, capc, blocked,
     ext_u, ext_y, et_u, et_y, ht_u, ht_y, above, below, zlow, cap, grad,
-    band_r, band_h, band_c, band_d, pick, plane_slots, layer_slots,
+    band_r, band_h, band_c, pick, slots,
     load_sem, send_sem, recv_sem, first_sem, zsend, zrecv, sum_sem,
 ):
     nl, nr, nc = sizes
     layers, rows, cols = x_in.shape
-    peers = nr * nc
+    ndev = nl * nr * nc
     il, ir, ic = lax.axis_index("layer"), lax.axis_index("row"), lax.axis_index("col")
-    me = ir * nc + ic
+    me = (il * nr + ir) * nc + ic
     tiles = rows // TILE
     order = list(dict.fromkeys((0, tiles - 1, *range(tiles))))
     inverse_area = 1.0 / (WIN * WIN)
@@ -80,22 +80,17 @@
 
     barrier = pltpu.get_barrier_semaphore()
 
-    def in_plane(act):
+    def others(act):
         def one(i, _):
-            pl.when(i != me)(lambda: act((il, i // nc, i % nc)))
+            pl.when(i != me)(lambda: act((i // (nr * nc), (i // nc) % nr, i % nc)))
             return 0
 
-        lax.fori_loop(0, peers, one, 0, unroll=peers <= 16)
-
-    def in_stack(act):
-        for i in range(nl):
-            pl.when(i != il)(lambda i=i: act((i, ir, ic)))
+        lax.fori_loop(0, ndev, one, 0, unroll=ndev <= 32)
 
     def greet(device):
         pl.semaphore_signal(barrier, inc=1, device_id=device, device_id_type=MESH)
 
-    in_plane(greet)
-    in_stack(greet)
+    others(greet)
 
     keep_top = jnp.where(il < nl - 1, 1.0, 0.0).astype(F32)
     keep_low = jnp.where(il > 0, 1.0, 0.0).astype(F32)
@@ -105,11 +100,19 @@
         shape = (TILE, 3 * TILE)
         band_h[which] = window(iota(shape, 1) - TILE - iota(shape, 0), start)
         shape = (cols, cols)
-        band_c[which] = window(iota(shape, 0) - iota(shape, 1), start)
+        inner = window(iota(shape, 0) - iota(shape, 1), start)
         shape = (2 * HALO, cols)
         k = iota(shape, 0)
         place = jnp.where(k < HALO, k - HALO, k - HALO + cols)
-        band_d[which] = window(place - iota(shape, 1), start)
+        outer = window(place - iota(shape, 1), start)
+        blank = jnp.zeros(shape, BF16)
+        half = cols + layers * 2 * HALO
+        for l in range(layers):
+            for base in (0, half):
+                band_c[which, l, base : base + cols] = inner
+                for m in range(layers):
+                    at = base + cols + m * 2 * HALO
+                    band_c[which, l, at : at + 2 * HALO] = outer if m == l else blank
     shape = (2 * HALO, cols)
     k = iota(shape, 0)
     place = jnp.where(k < HALO, k, k - 2 * HALO + cols)
@@ -119,15 +122,14 @@
         return pl.ds(t * TILE + base, TILE)
 
     def put_edges(et, l, t, value):
-        high, low = split(value)
-        et[l, :, span(t)] = dot(pick[...], high, NT) + dot(pick[...], low, NT)
+        et[l, :, span(t)] = dot(pick[...], value.astype(BF16), NT)
 
     loads[0].wait()
     for t in range(tiles):
         for l in range(layers):
             put_edges(et_y, l, t, ext_y[l, span(t, HALO), :])
 
-    pl.semaphore_wait(barrier, peers - 1 + nl - 1)
+    pl.semaphore_wait(barrier, ndev - 1)
 
     def copies(field):
         ext, et, ht = ((ext_u, et_u, ht_u), (ext_y, et_y, ht_y))[field]
@@ -205,26 +207,17 @@
             device_id=(il - 1, ir, ic), device_id_type=MESH,
         )
 
-    def inner(ext, which, l, t):
-        first = HALO if t == 0 else 0
-        end = TILE + HALO if t == tiles - 1 else TILE + 2 * HALO
-        high, low = split(ext[l, t * TILE + first : t * TILE + end, :])
-        band = band_r[which, :, first:end]
-        high, low = split(dot(band, high) + dot(band, low))
-        return dot(high, band_c[which]) + dot(low, band_c[which])
-
-    def outer(ext, ht, which, l, t):
-        high, low = split(ht[l, :, t * TILE : (t + 3) * TILE])
-        band = band_h[which]
-        high, low = split(dot(band, high, NT) + dot(band, low, NT))
-        total = dot(high, band_d[which]) + dot(low, band_d[which])
-        for edge, at, base in ((0, 0, 0), (tiles - 1, TILE + HALO, HALO + rows)):
-            if t == edge:
-                high, low = split(ext[l, base : base + HALO, :])
-                band = band_r[which, :, at : at + HALO]
-                high, low = split(dot(band, high) + dot(band, low))
-                total = total + dot(high, band_c[which]) + dot(low, band_c[which])
-        return total
+    def box(ext, ht, which, t):
+        tall = pl.ds(t * TILE, TILE + 2 * HALO)
+        wide = jnp.concatenate([ext[l, tall, :].astype(BF16) for l in range(layers)], axis=1)
+        mid = dot(band_r[which], wide)
+        halo = ht[:, :, t * TILE : (t + 3) * TILE].reshape(layers * 2 * HALO, 3 * TILE)
+        side = dot(band_h[which], halo.astype(BF16), NT)
+        result = []
+        for l in range(layers):
+            row = jnp.concatenate([mid[:, l * cols : (l + 1) * cols], side], axis=1)
+            result.append(dot(jnp.concatenate(split(row), axis=1), band_c[which, l]))
+        return result
 
     everywhere = [(l, t, (l, span(t), slice(None))) for t in order for l in range(layers)]
     for n in range(1, 7):
@@ -237,34 +230,26 @@
     def fold(value):
         return jnp.sum((value * value).reshape(TILE // 8, 8, cols), axis=0)
 
-    def sum_copy(slots, step, mine, stage, device):
-        return pltpu.make_async_remote_copy(
-            src_ref=slots.at[step, mine], dst_ref=slots.at[step, mine],
-            send_sem=sum_sem.at[stage, 0, step], recv_sem=sum_sem.at[stage, 1, step],
-            device_id=device, device_id_type=MESH,
-        )
-
-    def sums_wait(slots, step, stage, count):
-        if count > 1:
-            some = slots.at[step, pl.ds(0, count - 1)]
-            pltpu.make_async_copy(some, some, sum_sem.at[stage, 1, step]).wait()
-            pltpu.make_async_copy(some, some, sum_sem.at[stage, 0, step]).wait()
-
     def sums_begin(step, primal_sum, dual_sum):
-        plane_slots[step, pl.ds(me, 1)] = jnp.concatenate(
+        slots[step, pl.ds(me, 1)] = jnp.concatenate(
             [jnp.sum(primal_sum, axis=0, keepdims=True), jnp.sum(dual_sum, axis=0, keepdims=True)],
             axis=0,
         )[None]
-        in_plane(lambda device: sum_copy(plane_slots, step, me, 0, device).start())
-
-    def sums_forward(step):
-        sums_wait(plane_slots, step, 0, peers)
-        layer_slots[step, pl.ds(il, 1)] = jnp.sum(plane_slots[step], axis=0)[None]
-        in_stack(lambda device: sum_copy(layer_slots, step, il, 1, device).start())
+
+        def send(device):
+            pltpu.make_async_remote_copy(
+                src_ref=slots.at[step, me], dst_ref=slots.at[step, me],
+                send_sem=sum_sem.at[0, step], recv_sem=sum_sem.at[1, step],
+                device_id=device, device_id_type=MESH,
+            ).start()
+
+        others(send)
 
     def sums_end(step, weight):
-        sums_wait(layer_slots, step, 1, nl)
-        both = jnp.sum(layer_slots[step], axis=0)
+        some = slots.at[step, pl.ds(0, ndev - 1)]
+        pltpu.make_async_copy(some, some, sum_sem.at[1, step]).wait()
+        pltpu.make_async_copy(some, some, sum_sem.at[0, step]).wait()
+        both = jnp.sum(slots[step], axis=0)
         primal = jnp.sum(both[0:1], axis=1, keepdims=True)
         dual = jnp.sum(both[1:2], axis=1, keepdims=True)
         ratio = jnp.broadcast_to((dual + tiny_term) / (primal + tiny_term), (1, cols))
@@ -273,17 +258,15 @@
     weight = jnp.ones((1, cols), F32)
     for step in range(ITERS):
         last = step == ITERS - 1
-        for l, t, at in everywhere:
-            grad[at] = cost[at] + inner(ext_y, 1, l, t) * inverse_area
-        if step > 0:
-            sums_forward(step - 1)
-        else:
+        if step == 0:
             pl.when(has_below)(first_up.wait_recv)
             pl.when(has_above)(first_up.wait_send)
         finish(1)
-        for l, t, at in everywhere:
-            earlier = zlow[span(t), :] if l == 0 else z[l - 1, span(t), :]
-            grad[at] = grad[at] + outer(ext_y, ht_y, 1, l, t) * inverse_area + (z[at] - earlier)
+        for t in order:
+            for l, area in enumerate(box(ext_y, ht_y, 1, t)):
+                at = (l, span(t), slice(None))
+                earlier = zlow[span(t), :] if l == 0 else z[l - 1, span(t), :]
+                grad[at] = cost[at] + area * inverse_area + (z[at] - earlier)
         if step > 0:
             weight = sums_end(step - 1, weight)
         tau = step_eta / weight
@@ -307,14 +290,15 @@
                 if t == order[min(1, tiles - 1)]:
                     begin(0, EDGE)
         begin(0, SIDE)
+        finish(0)
+
+        dual_sum = jnp.zeros((8, cols), F32)
+        areas = {}
         for l, t, at in everywhere:
-            grad[at] = inner(ext_u, 0, l, t)
-        finish(0)
-
-        dual_sum = jnp.zeros((8, cols), F32)
-        for l, t, at in everywhere:
+            if l == 0:
+                areas = box(ext_u, ht_u, 0, t)
             old = ext_y[l, span(t, HALO), :]
-            term = old * sigma_inverse + (grad[at] + outer(ext_u, ht_u, 0, l, t)) * inverse_area
+            term = old * sigma_inverse + areas[l] * inverse_area
             capped = jnp.minimum(term, high_density)
             clipped = jnp.where(blocked[at] == 0, jnp.maximum(capped, low_density), capped)
             new = sigma * (term - clipped)
@@ -350,13 +334,12 @@
                 zlow[span(t), :] = update(zlow[span(t), :], below[span(t), :], levels[0], keep_low)
         sums_begin(step, primal_sum, dual_sum)
 
-    sums_forward(ITERS - 1)
     weight_out[...] = sums_end(ITERS - 1, weight)
 
 
 def local(sizes, *args):
     layers, rows, cols = args[0].shape
-    peers = sizes[1] * sizes[2]
+    ndev = sizes[0] * sizes[1] * sizes[2]
     tiles = rows // TILE
     whole = jax.ShapeDtypeStruct((layers, rows, cols), F32)
     vmem = pl.BlockSpec(memory_space=pltpu.VMEM)
@@ -378,18 +361,16 @@
             ext, ext, et, et, ht, ht, plane, plane, plane, full, full,
             pltpu.VMEM((2, TILE, TILE + 2 * HALO), BF16),
             pltpu.VMEM((2, TILE, 3 * TILE), BF16),
-            pltpu.VMEM((2, cols, cols), BF16),
-            pltpu.VMEM((2, 2 * HALO, cols), BF16),
+            pltpu.VMEM((2, layers, 2 * (cols + layers * 2 * HALO), cols), BF16),
             pltpu.VMEM((2 * HALO, cols), BF16),
-            pltpu.VMEM((ITERS, peers, 2, cols), F32),
-            pltpu.VMEM((ITERS, sizes[0], 2, cols), F32),
+            pltpu.VMEM((ITERS, ndev, 2, cols), F32),
             pltpu.SemaphoreType.DMA((7,)),
             pltpu.SemaphoreType.DMA((2, 8)),
             pltpu.SemaphoreType.DMA((2, 8)),
             pltpu.SemaphoreType.DMA((2,)),
             pltpu.SemaphoreType.DMA((2, tiles)),
             pltpu.SemaphoreType.DMA((2, tiles)),
-            pltpu.SemaphoreType.DMA((2, 2, ITERS)),
+            pltpu.SemaphoreType.DMA((2, ITERS)),
         ],
         compiler_params=pltpu.CompilerParams(collective_id=0, has_side_effects=True),
         name="fill_steps",

time: 64 us -> 56.3 us (0.88)
  Pallas kernels: 59.7 us -> 51.9 us
    pallas_call x1, Pallas kernels: 59.7 us -> 51.9 us  [local(): pl.pallas_call(functools.partial(kernel, sizes), out_shape=(full, full, f...]
where the time goes in v3:
time: 56.3 us; the launch traced here: 56.1 us
  Pallas kernels  51.9 us (92%)
  local copies, waits for them, and re-layouts  2.38 us (4%)
  between operations  1.81 us (3%)
    pallas_call x1, Pallas kernels, local(): pl.pallas_call(functools.partial(kernel, sizes), out_shape=(full, full, f...  51.9 us
    unnamed x3, local copies, waits for them, and re-layouts  2.38 us

profile of v3, /device:TPU:0, one launch (start us, length us, event | category | flops | bytes accessed | tf_op | source)
XLA Modules:
  0.0 56.1 jit_solution(1745573783401668142)
XLA Ops:
  0.6 51.9 %fill_steps.1 = (f32[2,512,128]{2,1,0:T(8,128)S(1)}, f32[2,512,128]{2,1,0:T(8,128)S(1)}, f32[2,512,128]{2,1,0:T(8,128)S(1)}, f32[1,128]{1,0:T(1,128)S(1)}) custom-call(f32[2,512,128]{2,1,0:T(8,128)} %cost_in.1, f32[2,512,128]{2,1,0:T(8,128)} %dens_in.1, s32[2,512,128]{2,1,0:T(8,128)} %capc_in.1, s32[2,512,128]{2,1,0:T(8,128)} %blocked_in.1, ...), custom_call_target="tpu_custom_call" | custom-call | tf_op jit(solution)/shard_map/fill_steps/pallas_call | solution.py:354
  52.6 0.8 %copy.15 = f32[2,512,128]{2,1,0:T(8,128)} copy(f32[2,512,128]{2,1,0:T(8,128)S(1)} %get-tuple-element.12) | data formatting | bytes 1048576
  53.4 0.8 %copy.16 = f32[2,512,128]{2,1,0:T(8,128)} copy(f32[2,512,128]{2,1,0:T(8,128)S(1)} %get-tuple-element.13) | data formatting | bytes 1048576
  54.1 0.8 %copy.17 = f32[2,512,128]{2,1,0:T(8,128)} copy(f32[2,512,128]{2,1,0:T(8,128)S(1)} %get-tuple-element.14) | data formatting | bytes 1048576

commit v4 on v3

--- a/solution.py
+++ b/solution.py
@@ -52,7 +52,7 @@
     cost, dens, capc, blocked,
     ext_u, ext_y, et_u, et_y, ht_u, ht_y, above, below, zlow, cap, grad,
     band_r, band_h, band_c, pick, slots,
-    load_sem, send_sem, recv_sem, first_sem, zsend, zrecv, sum_sem,
+    load_sem, send_sem, recv_sem, first_sem, zsend, zrecv, sum_sem, zhigh, tsend, trecv,
 ):
     nl, nr, nc = sizes
     layers, rows, cols = x_in.shape
@@ -75,7 +75,7 @@
     for ref in (ext_u, ext_y):
         ref[:, :HALO, :] = jnp.zeros((layers, HALO, cols), F32)
         ref[:, HALO + rows :, :] = jnp.zeros((layers, HALO, cols), F32)
-    for ref in (ht_u, ht_y, above, below, zlow):
+    for ref in (ht_u, ht_y, above, below, zlow, zhigh):
         ref[...] = jnp.zeros(ref.shape, F32)
 
     barrier = pltpu.get_barrier_semaphore()
@@ -207,6 +207,32 @@
             device_id=(il - 1, ir, ic), device_id_type=MESH,
         )
 
+    lower, upper = order[0::2], order[1::2]
+
+    def give_up(t):
+        return pltpu.make_async_remote_copy(
+            src_ref=z.at[layers - 1, span(t), :], dst_ref=zlow.at[span(t), :],
+            send_sem=tsend.at[t], recv_sem=trecv.at[t],
+            device_id=(il + 1, ir, ic), device_id_type=MESH,
+        )
+
+    def give_down(t):
+        return pltpu.make_async_remote_copy(
+            src_ref=zlow.at[span(t), :], dst_ref=zhigh.at[span(t), :],
+            send_sem=tsend.at[t], recv_sem=trecv.at[t],
+            device_id=(il - 1, ir, ic), device_id_type=MESH,
+        )
+
+    def take(last):
+        for t in upper:
+            pl.when(has_above)(give_down(t).wait_recv)
+            pl.when(has_below)(give_down(t).wait_send)
+            z[layers - 1, span(t), :] = zhigh[span(t), :]
+        if not last:
+            for t in lower:
+                pl.when(has_below)(give_up(t).wait_recv)
+                pl.when(has_above)(give_up(t).wait_send)
+
     def box(ext, ht, which, t):
         tall = pl.ds(t * TILE, TILE + 2 * HALO)
         wide = jnp.concatenate([ext[l, tall, :].astype(BF16) for l in range(layers)], axis=1)
@@ -262,6 +288,8 @@
             pl.when(has_below)(first_up.wait_recv)
             pl.when(has_above)(first_up.wait_send)
         finish(1)
+        if step > 0:
+            take(False)
         for t in order:
             for l, area in enumerate(box(ext_y, ht_y, 1, t)):
                 at = (l, span(t), slice(None))
@@ -284,9 +312,10 @@
             ext_u[l, span(t, HALO), :] = value
             put_edges(et_u, l, t, value)
             if l == layers - 1:
-                if not last:
+                if t in upper:
                     pl.when(has_above)(up(t).start)
-                pl.when(has_below)(down(t).start)
+                else:
+                    pl.when(has_below)(down(t).start)
                 if t == order[min(1, tiles - 1)]:
                     begin(0, EDGE)
         begin(0, SIDE)
@@ -318,22 +347,34 @@
             return sigma * (term - jnp.clip(term, -layer_gap, layer_gap)) * keep
 
         for t in order:
-            pl.when(has_above)(down(t).wait_recv)
-            pl.when(has_below)(down(t).wait_send)
-            if not last:
+            levels = [ext_u[l, span(t, HALO), :] for l in range(layers)]
+            for l in range(layers - 1):
+                at = (l, span(t), slice(None))
+                old = z[at]
+                new = update(old, levels[l], levels[l + 1], 1.0)
+                z[at] = new
+                dual_sum = dual_sum + fold(new - old)
+            if t in lower:
+                pl.when(has_above)(down(t).wait_recv)
+                pl.when(has_below)(down(t).wait_send)
+                old = z[layers - 1, span(t), :]
+                new = update(old, levels[layers - 1], above[span(t), :], keep_top)
+                z[layers - 1, span(t), :] = new
+            else:
                 pl.when(has_below)(up(t).wait_recv)
                 pl.when(has_above)(up(t).wait_send)
-            levels = [ext_u[l, span(t, HALO), :] for l in range(layers)] + [above[span(t), :]]
-            for l in range(layers):
-                at = (l, span(t), slice(None))
-                old = z[at]
-                new = update(old, levels[l], levels[l + 1], keep_top if l == layers - 1 else 1.0)
-                z[at] = new
-                dual_sum = dual_sum + fold(new - old)
-            if not last:
-                zlow[span(t), :] = update(zlow[span(t), :], below[span(t), :], levels[0], keep_low)
+                old = zlow[span(t), :]
+                new = update(old, below[span(t), :], levels[0], keep_low)
+                zlow[span(t), :] = new
+            dual_sum = dual_sum + fold(new - old)
         sums_begin(step, primal_sum, dual_sum)
-
+        for t in order:
+            if t in upper:
+                pl.when(has_below)(give_down(t).start)
+            elif not last:
+                pl.when(has_above)(give_up(t).start)
+
+    take(True)
     weight_out[...] = sums_end(ITERS - 1, weight)
 
 
@@ -371,6 +412,9 @@
             pltpu.SemaphoreType.DMA((2, tiles)),
             pltpu.SemaphoreType.DMA((2, tiles)),
             pltpu.SemaphoreType.DMA((2, ITERS)),
+            plane,
+            pltpu.SemaphoreType.DMA((tiles,)),
+            pltpu.SemaphoreType.DMA((tiles,)),
         ],
         compiler_params=pltpu.CompilerParams(collective_id=0, has_side_effects=True),
         name="fill_steps",

time: 56.3 us -> 57.1 us (1.014)
  Pallas kernels: 51.9 us -> 52.7 us
    pallas_call x1, Pallas kernels: 51.9 us -> 52.7 us  [local(): pl.pallas_call(functools.partial(kernel, sizes), out_shape=(full, full, f...]
where the time goes in v4:
time: 57.1 us; the launch traced here: 56.9 us
  Pallas kernels  52.7 us (92%)
  local copies, waits for them, and re-layouts  2.38 us (4%)
  between operations  1.81 us (3%)
    pallas_call x1, Pallas kernels, local(): pl.pallas_call(functools.partial(kernel, sizes), out_shape=(full, full, f...  52.7 us
    unnamed x3, local copies, waits for them, and re-layouts  2.38 us

profile of v4, /device:TPU:0, one launch (start us, length us, event | category | flops | bytes accessed | tf_op | source)
XLA Modules:
  0.0 56.9 jit_solution(17095591453770084877)
XLA Ops:
  0.6 52.7 %fill_steps.1 = (f32[2,512,128]{2,1,0:T(8,128)S(1)}, f32[2,512,128]{2,1,0:T(8,128)S(1)}, f32[2,512,128]{2,1,0:T(8,128)S(1)}, f32[1,128]{1,0:T(1,128)S(1)}) custom-call(f32[2,512,128]{2,1,0:T(8,128)} %cost_in.1, f32[2,512,128]{2,1,0:T(8,128)} %dens_in.1, s32[2,512,128]{2,1,0:T(8,128)} %capc_in.1, s32[2,512,128]{2,1,0:T(8,128)} %blocked_in.1, ...), custom_call_target="tpu_custom_call" | custom-call | tf_op jit(solution)/shard_map/fill_steps/pallas_call | solution.py:395
  53.4 0.8 %copy.15 = f32[2,512,128]{2,1,0:T(8,128)} copy(f32[2,512,128]{2,1,0:T(8,128)S(1)} %get-tuple-element.12) | data formatting | bytes 1048576
  54.2 0.8 %copy.16 = f32[2,512,128]{2,1,0:T(8,128)} copy(f32[2,512,128]{2,1,0:T(8,128)S(1)} %get-tuple-element.13) | data formatting | bytes 1048576
  55.0 0.8 %copy.17 = f32[2,512,128]{2,1,0:T(8,128)} copy(f32[2,512,128]{2,1,0:T(8,128)S(1)} %get-tuple-element.14) | data formatting | bytes 1048576
